TPU v7x, 512 devices: a whole 4x4x16 slice. The times are simulated.
512 devices in a mesh: space: 32 (over z, x_lo), chan: 16 (over x_hi, y, core).
Axes of the slice: x: 4 (x_hi: 2, x_lo: 2; x = x_hi * 2 + x_lo), y: 4, z: 16, core: 2. Of those that a mesh axis runs over, the one named last changes fastest.
Arguments:
- volume: bfloat16 [64, 256, 8, 128], P('space', 'chan'), may hold values from -6 to 6
- kernel: bfloat16 [27, 256, 256], P(None, 'chan'), may hold values from -0.078125 to 0.078125
- cotangent: bfloat16 [64, 256, 8, 128], P('space', 'chan'), may hold values from -6 to 6
Outputs:
- output_map: bfloat16 [64, 256, 8, 128], P('space', 'chan')
- input_grad: bfloat16 [64, 256, 8, 128], P('space', 'chan')
- kernel_grad: float32 [27, 256, 256], P(None, 'chan')
All inputs are finite; a program needn't handle non-finite values.
Results may differ from a plain program's by a relative error of at most 0.001.
Values may be sent and summed in bfloat16 or wider, within the bound.
A program may use at most 128 MiB of HBM per device.

v0:
```python
import math
import jax
import jax.numpy as jnp
from jax import lax
from jax.sharding import PartitionSpec as P


def with_halo(block, sides, width):
    for axis, dim in sides:
        count = lax.axis_size(axis)
        forward = [(i, i + 1) for i in range(count - 1)]
        backward = [(target, source) for source, target in forward]
        low = lax.ppermute(
            lax.slice_in_dim(block, block.shape[dim] - width, None, axis=dim), axis, forward
        )
        high = lax.ppermute(lax.slice_in_dim(block, 0, width, axis=dim), axis, backward)
        block = jnp.concatenate([low, block, high], axis=dim)
    return block


def plane_stack(piece, height, width, flipped):
    cells = height * width
    padded = jnp.pad(piece, ((0, 0), (0, 0), (width + 1, width + 1)))
    column = lax.broadcasted_iota(jnp.int32, (1, 1, cells), 2) % width
    windows = []
    for row_step in range(3):
        for col_step in range(3):
            row_from = 2 - row_step if flipped else row_step
            col_from = 2 - col_step if flipped else col_step
            offset = width + 1 + (row_from - 1) * width + (col_from - 1)
            shifted = padded[:, :, offset : offset + cells]
            target = column + (col_from - 1)
            inside = ((target >= 0) & (target < width)).astype(piece.dtype)
            windows.append(shifted * inside)
    return jnp.concatenate(windows, axis=1)


def on_device(volume, kernel, cotangent):
    depth, chans_local, height, width = volume.shape
    filters_local = cotangent.shape[1]
    cells = height * width
    scale_factor = 1.0 / math.sqrt(depth * lax.axis_size("space") * height * width)
    volume_flat = volume.reshape(depth, chans_local, cells)
    grad_flat = cotangent.reshape(depth, filters_local, cells)
    columns = lax.all_to_all(kernel, "chan", split_axis=2, concat_axis=1, tiled=True)
    init_output = jnp.zeros((depth, filters_local, cells), jnp.float32)
    init_input = jnp.zeros((depth, chans_local, cells), jnp.float32)
    rims = with_halo(volume_flat, (("space", 0),), 1)
    piece = lax.all_gather(rims, "chan", axis=1, tiled=True)
    output_acc = init_output
    count = piece.shape[1]
    stacked = plane_stack(piece, height, width, False)
    grads = []
    for depth_step in range(3):
        window = stacked[depth_step : depth_step + depth]
        taps = kernel[9 * depth_step : 9 * depth_step + 9]
        weights = jnp.transpose(taps, (1, 0, 2)).reshape(filters_local, 9 * count)
        output_acc = output_acc + jnp.einsum(
            "fj,zjp->zfp", weights, window, preferred_element_type=jnp.float32
        )
        term = jnp.einsum("zfp,zjp->fj", grad_flat, window, preferred_element_type=jnp.float32)
        grads.append(jnp.transpose(term.reshape(filters_local, 9, count), (1, 0, 2)))
    kernel_acc = jnp.concatenate(grads, axis=0)
    output_acc, kernel_acc = (output_acc, kernel_acc)
    grad_ext = with_halo(grad_flat, (("space", 0),), 1)
    total = init_input
    piece = lax.all_gather(grad_ext, "chan", axis=1, tiled=True)
    count = piece.shape[1]
    stacked = plane_stack(piece, height, width, True)
    for depth_step in range(3):
        window = stacked[2 - depth_step : 2 - depth_step + depth]
        taps = columns[9 * depth_step : 9 * depth_step + 9]
        weights = jnp.transpose(taps, (2, 0, 1)).reshape(chans_local, 9 * count)
        total = total + jnp.einsum(
            "kj,zjp->zkp", weights, window, preferred_element_type=jnp.float32
        )
    kernel_grad = lax.psum(kernel_acc, "space") * scale_factor
    output_map = output_acc.astype(jnp.bfloat16).reshape(depth, filters_local, height, width)
    input_grad = total.astype(jnp.bfloat16).reshape(depth, chans_local, height, width)
    return (output_map, input_grad, kernel_grad)


def solution(mesh):
    return jax.shard_map(
        on_device,
        mesh=mesh,
        in_specs=(
            P("space", "chan", None, None),
            P(None, "chan", None),
            P("space", "chan", None, None),
        ),
        out_specs=(
            P("space", "chan", None, None),
            P("space", "chan", None, None),
            P(None, "chan", None),
        ),
        check_vma=False,
    )
```

profile of v0, /device:TPU:8, one launch (start us, length us, event | category | flops | bytes accessed | tf_op | source)
XLA Modules:
  0.0 456.1 jit_solution(4387820770311451748)
XLA Ops:
  8.1 3.4 collective-permute-start.2
  13.7 3.6 collective-permute-done.3
  18.9 4.7 %collective-permute-start = (bf16[1,16,1024]{2,1,0:T(8,128)(2,1)S(1)}, bf16[1,16,1024]{2,1,0:T(8,128)(2,1)S(1)}, u32[]{:S(2)}, u32[]{:S(2)}) collective-permute-start(bf16[1,16,1024]{2,1,0:T(8,128)(2,1)S(1)} %slice.120), channel_id=1, source_target_pairs={{0,16},{16,32},{32,48},{48,64},{64,80},{80,96},{96,112},{112,128},... | collective-permute-start | bytes 98312 | tf_op jit(solution)/shard_map/ppermute | solution.py:13
  25.8 3.6 collective-permute-done.1
  30.1 2.0 copy.40
  32.1 2.5 reshape.125
  34.6 7.4 %all-to-all-start = ((bf16[16,2,3456]{2,1,0:T(2,128)(2,1)}), bf16[16,2,3456]{2,1,0:T(2,128)(2,1)S(1)}, u32[]{:S(2)}, u32[]{:S(2)}) async-start(bf16[16,2,3456]{2,1,0:T(2,128)(2,1)} %reshape.125), calls=%async_computation | async-start | bytes 442368 | tf_op jit(solution)/shard_map/all_to_all | solution.py:45
  44.3 5.4 %all-to-all-done = bf16[16,2,3456]{2,1,0:T(2,128)(2,1)S(1)} async-done(((bf16[16,2,3456]{2,1,0:T(2,128)(2,1)}), bf16[16,2,3456]{2,1,0:T(2,128)(2,1)S(1)}, u32[]{:S(2)}, u32[]{:S(2)}) %all-to-all-start) | async-done | bytes 221216 | tf_op jit(solution)/shard_map/all_to_all | solution.py:45
  49.6 2.7 reshape.126
  52.3 4.2 copy.49
  61.3 26.4 %all-gather.5.cloned.1.call-done = bf16[4,256,1024]{2,1,0:T(8,128)(2,1)} async-done(((bf16[4,16,1024]{2,1,0:T(8,128)(2,1)}), bf16[4,256,1024]{2,1,0:T(8,128)(2,1)}) %all-gather.5.cloned.1.call-update) | async-done | bytes 2097168 | tf_op jit(solution)/shard_map/all_gather | solution.py:67
  87.7 3.8 fusion.29
  91.5 1.9 fusion.31
  93.3 2.6 fusion.33
  95.9 2.6 fusion.35
  98.5 1.9 multiply_dynamic-update-slice_fusion
  100.4 52.5 %all-gather.3.cloned.1.call-done = bf16[4,256,1024]{2,1,0:T(8,128)(2,1)} async-done(((bf16[4,16,1024]{2,1,0:T(8,128)(2,1)}), bf16[4,256,1024]{2,1,0:T(8,128)(2,1)}) %all-gather.3.cloned.1.call-update) | async-done | bytes 2097168 | tf_op jit(solution)/shard_map/all_gather | solution.py:49
  152.9 4.5 fusion.37
  157.3 2.7 fusion.39
  160.0 2.4 fusion.41
  162.4 1.3 fusion.17
  163.7 3.9 fusion.43
  172.4 2.5 convolution_bitcast_fusion.2
  175.0 2.8 convolution_bitcast_fusion.1
  178.8 2.5 convolution_bitcast_fusion
  182.4 5.0 %fusion = f32[2,1024,16]{1,2,0:T(8,128)S(1)} fusion(bf16[16,2304,1]{1,0,2:T(8,128)(2,1)S(1)} %reshape.115, bf16[4,2304,1024]{2,1,0:T(8,128)(2,1)} %get-tuple-element.22), kind=kOutput, calls=%fused_computation | convolution fusion | flops 150994944 | bytes 9641984 | tf_op jit(solution)/shard_map/kj,zjp->zkp/dot_general | solution.py:74
  187.4 5.2 %fusion.2 = f32[2,1024,16]{1,2,0:T(8,128)S(1)} fusion(bf16[16,2304,1]{1,0,2:T(8,128)(2,1)S(1)} %reshape.114, bf16[4,2304,1024]{2,1,0:T(8,128)(2,1)} %get-tuple-element.22), kind=kOutput, calls=%fused_computation.2 | convolution fusion | flops 150994944 | bytes 9641984 | tf_op jit(solution)/shard_map/kj,zjp->zkp/dot_general | solution.py:74
  192.6 5.8 %fusion.56 = bf16[2,1024,16]{1,2,0:T(8,128)(2,1)S(1)} fusion(f32[2,1024,16]{1,2,0:T(8,128)S(1)} %fusion, f32[2,1024,16]{1,2,0:T(8,128)S(1)} %fusion.2, bf16[16,2304,1]{1,0,2:T(8,128)(2,1)S(1)} %reshape.113, bf16[4,2304,1024]{2,1,0:T(8,128)(2,1)} %get-tuple-element.22), kind=kOutput, calls=%fused_computation.69 | convolution fusion | flops 151093248 | bytes 9838592 | tf_op jit(solution)/shard_map/kj,zjp->zkp/dot_general | solution.py:74
  199.3 1.3 fusion.8
  200.6 1.3 fusion.6
  202.0 1.3 fusion.59
  204.0 243.3 %all-reduce.4.cloned.1.call-done = f32[27,16,256]{2,0,1:T(8,128)} async-done(((f32[27,16,256]{2,0,1:T(8,128)}), f32[27,16,256]{2,0,1:T(8,128)}) %all-reduce.4.cloned.1.call-update) | async-done | bytes 442384 | tf_op jit(solution)/shard_map/psum | solution.py:77
  (76 shorter events, 24.8 us)
Async XLA Ops:
  7.2 34.9 %copy-start.6 = (bf16[27,16,256]{2,1,0:T(8,128)(2,1)S(1)}, bf16[27,16,256]{2,1,0:T(8,128)(2,1)}, u32[]{:S(2)}) copy-start(bf16[27,16,256]{2,1,0:T(8,128)(2,1)} %param.4) | copy-start | bytes 663556
  7.2 80.5 %all-gather.5.cloned.1.call-start = ((), (), s32[]{:S(2)}) async-start(), calls=%async_computation.2 | async-start | bytes 2228224 | tf_op jit(solution)/shard_map/all_gather | solution.py:67
  8.1 5.6 %collective-permute-start.2 = (bf16[1,16,1024]{2,1,0:T(8,128)(2,1)S(1)}, bf16[1,16,1024]{2,1,0:T(8,128)(2,1)S(1)}, u32[]{:S(2)}, u32[]{:S(2)}) collective-permute-start(bf16[1,16,1024]{2,1,0:T(8,128)(2,1)S(1)} %slice.138), channel_id=1, source_target_pairs={{0,16},{16,32},{32,48},{48,64},{64,80},{80,96},{96,112},{112,128},... | collective-permute-start | bytes 98312 | tf_op jit(solution)/shard_map/ppermute | solution.py:13
  11.5 5.8 %collective-permute-start.3 = (bf16[1,16,1024]{2,1,0:T(8,128)(2,1)S(1)}, bf16[1,16,1024]{2,1,0:T(8,128)(2,1)S(1)}, u32[]{:S(2)}, u32[]{:S(2)}) collective-permute-start(bf16[1,16,1024]{2,1,0:T(8,128)(2,1)S(1)} %slice.140), channel_id=1, source_target_pairs={{16,0},{32,16},{48,32},{64,48},{80,64},{96,80},{112,96},{128,112},... | collective-permute-start | bytes 98312 | tf_op jit(solution)/shard_map/ppermute | solution.py:16
  13.7 16.4 %copy-start.4 = (bf16[2,16,1024]{2,1,0:T(8,128)(2,1)}, bf16[2,16,1024]{2,1,0:T(8,128)(2,1)S(1)}, u32[]{:S(2)}) copy-start(bf16[2,16,1024]{2,1,0:T(8,128)(2,1)S(1)} %reshape.102) | copy-start | bytes 196612
  18.0 134.9 %all-gather.3.cloned.1.call-start = ((), (), s32[]{:S(2)}) async-start(), calls=%async_computation.1 | async-start | bytes 2228224 | tf_op jit(solution)/shard_map/all_gather | solution.py:49
  18.9 6.9 %collective-permute-start = (bf16[1,16,1024]{2,1,0:T(8,128)(2,1)S(1)}, bf16[1,16,1024]{2,1,0:T(8,128)(2,1)S(1)}, u32[]{:S(2)}, u32[]{:S(2)}) collective-permute-start(bf16[1,16,1024]{2,1,0:T(8,128)(2,1)S(1)} %slice.120), channel_id=1, source_target_pairs={{0,16},{16,32},{32,48},{48,64},{64,80},{80,96},{96,112},{112,128},... | collective-permute-start | bytes 98312 | tf_op jit(solution)/shard_map/ppermute | solution.py:13
  23.6 5.8 %collective-permute-start.1 = (bf16[1,16,1024]{2,1,0:T(8,128)(2,1)S(1)}, bf16[1,16,1024]{2,1,0:T(8,128)(2,1)S(1)}, u32[]{:S(2)}, u32[]{:S(2)}) collective-permute-start(bf16[1,16,1024]{2,1,0:T(8,128)(2,1)S(1)} %slice.122), channel_id=1, source_target_pairs={{16,0},{32,16},{48,32},{64,48},{80,64},{96,80},{112,96},{128,112},... | collective-permute-start | bytes 98312 | tf_op jit(solution)/shard_map/ppermute | solution.py:16
  34.6 15.0 %all-to-all-start = ((bf16[16,2,3456]{2,1,0:T(2,128)(2,1)}), bf16[16,2,3456]{2,1,0:T(2,128)(2,1)S(1)}, u32[]{:S(2)}, u32[]{:S(2)}) async-start(bf16[16,2,3456]{2,1,0:T(2,128)(2,1)} %reshape.125), calls=%async_computation | async-start | bytes 442368 | tf_op jit(solution)/shard_map/all_to_all | solution.py:45
  42.0 405.2 %all-reduce.4.cloned.1.call-start = ((), (), s32[]{:S(2)}) async-start(), calls=%async_computation.3 | async-start | bytes 1048576 | tf_op jit(solution)/shard_map/psum | solution.py:77
  87.7 3.8 copy-start.2
  157.3 2.7 copy-start.3
  170.8 1.6 copy-start.5
  172.4 6.4 %copy-start = (bf16[4,2304,1024]{2,1,0:T(8,128)(2,1)}, bf16[4,2304,1024]{2,1,0:T(8,128)(2,1)S(1)}, u32[]{:S(2)}) copy-start(bf16[4,2304,1024]{2,1,0:T(8,128)(2,1)S(1)} %fusion.27) | copy-start | bytes 56623108
  187.4 11.8 %copy-start.1 = (bf16[4,2304,1024]{2,1,0:T(8,128)(2,1)S(1)}, bf16[4,2304,1024]{2,1,0:T(8,128)(2,1)}, u32[]{:S(2)}) copy-start(bf16[4,2304,1024]{2,1,0:T(8,128)(2,1)} %copy-done) | copy-start | bytes 56623108
  192.6 6.7 %copy-start.7 = (bf16[16,2304,1]{1,0,2:T(8,128)(2,1)S(1)}, bf16[16,2304,1]{1,0,2:T(8,128)(2,1)}, u32[]{:S(2)}) copy-start(bf16[16,2304,1]{1,0,2:T(8,128)(2,1)} %reshape.111) | copy-start | bytes 221188
  199.3 1.3 copy-start.8
  200.6 1.4 copy-start.9
Sparse Core Ops, SparseCore 0:
  18.1 69.4 all-gather.4
  91.1 61.7 all-gather.2
  182.5 264.7 all-reduce.3
where the time goes:
time: 462 us; the launch traced here: 456 us
  waiting for transfers between devices  335 us (73%)
  other arithmetic  35.5 us (8%)
  matrix products  27.8 us (6%)
  local copies, waits for them, and re-layouts  25.5 us (6%)
  starting transfers between devices  18.2 us (4%)
  between operations  14.3 us (3%)
    psum x1, waiting for transfers between devices, on_device(): kernel_grad = lax.psum(kernel_acc, 'space') * scale_factor  243 us
    all_gather x1, waiting for transfers between devices, on_device(): piece = lax.all_gather(rims, 'chan', axis=1, tiled=True)  52.5 us
    unnamed x13, other arithmetic  27.2 us
    all_gather x1, waiting for transfers between devices, on_device(): piece = lax.all_gather(grad_ext, 'chan', axis=1, tiled=True)  26.4 us
    dot_general x3, matrix products, on_device(): jnp.einsum('kj,zjp->zkp', weights, window, preferred_element_type=jnp.flo...  16 us
    unnamed x26, local copies, waits for them, and re-layouts  10.9 us
  transfers between devices with their start and end apart: 8, of which 6 were waited for; matrix products, arithmetic and copies ran while one was open for 12% of the time, Pallas kernels for 0%

commit v1 on v0

--- a/solution.py
+++ b/solution.py
@@ -3,6 +3,11 @@
 import jax.numpy as jnp
 from jax import lax
 from jax.sharding import PartitionSpec as P
+
+
+def gather_over(x, mesh_axis, dim):
+    stack = jnp.stack([x] * lax.axis_size(mesh_axis))
+    return jnp.concatenate(lax.all_to_all(stack, mesh_axis, 0, 0), axis=dim)
 
 
 def with_halo(block, sides, width):
@@ -46,7 +51,7 @@
     init_output = jnp.zeros((depth, filters_local, cells), jnp.float32)
     init_input = jnp.zeros((depth, chans_local, cells), jnp.float32)
     rims = with_halo(volume_flat, (("space", 0),), 1)
-    piece = lax.all_gather(rims, "chan", axis=1, tiled=True)
+    piece = gather_over(rims, "chan", 1)
     output_acc = init_output
     count = piece.shape[1]
     stacked = plane_stack(piece, height, width, False)

time: 462 us -> 414 us (0.90)
  waiting for transfers between devices: 335 us -> 268 us
  local copies, waits for them, and re-layouts: 25.5 us -> 44.8 us
  other arithmetic: 35.5 us -> 27.2 us
  starting transfers between devices: 18.2 us -> 25.4 us
    all_gather x1 -> x0, waiting for transfers between devices: 52.5 us -> none  [on_device(): piece = lax.all_gather(rims, 'chan', axis=1, tiled=True)]
    all_gather x1, waiting for transfers between devices: 26.4 us -> 4.98 us  [on_device(): piece = lax.all_gather(grad_ext, 'chan', axis=1, tiled=True)]
    all_to_all x0 -> x1, waiting for transfers between devices: none -> 8.87 us  [gather_over(): return jnp.concatenate(lax.all_to_all(stack, mesh_axis, 0, 0), axis=dim)]
    unnamed x26 -> x28, local copies, waits for them, and re-layouts: 10.9 us -> 19.5 us
    unnamed x13, other arithmetic: 27.2 us -> 19 us
    all_to_all x0 -> x1, starting transfers between devices: none -> 7.83 us  [gather_over(): return jnp.concatenate(lax.all_to_all(stack, mesh_axis, 0, 0), axis=dim)]
    slice x7, local copies, waits for them, and re-layouts: 4.45 us -> 11.3 us  [on_device(): taps = columns[9 * depth_step:9 * depth_step + 9]]
    all_to_all x1, waiting for transfers between devices: 5.36 us -> 0.01 us  [on_device(): lax.all_to_all(kernel, 'chan', split_axis=2, concat_axis=1, tiled=True)]
  transfers between devices with their start and end apart: 8 -> 8, of which waited for: 6 -> 5; matrix products, arithmetic and copies ran while one was open for 12% -> 13% of each run, Pallas kernels for 0% -> 0%
where the time goes in v1:
time: 414 us; the launch traced here: 408 us
  waiting for transfers between devices  268 us (65%)
  local copies, waits for them, and re-layouts  44.8 us (11%)
  matrix products  27.8 us (7%)
  other arithmetic  27.2 us (7%)
  starting transfers between devices  25.4 us (6%)
  between operations  14.7 us (4%)
    psum x1, waiting for transfers between devices, on_device(): kernel_grad = lax.psum(kernel_acc, 'space') * scale_factor  247 us
    unnamed x28, local copies, waits for them, and re-layouts  19.5 us
    unnamed x13, other arithmetic  19 us
    dot_general x3, matrix products, on_device(): jnp.einsum('kj,zjp->zkp', weights, window, preferred_element_type=jnp.flo...  16 us
    slice x7, local copies, waits for them, and re-layouts, on_device(): taps = columns[9 * depth_step:9 * depth_step + 9]  11.3 us
    all_to_all x1, waiting for transfers between devices, gather_over(): return jnp.concatenate(lax.all_to_all(stack, mesh_axis, 0, 0), axis=dim)  8.87 us
  transfers between devices with their start and end apart: 8, of which 5 were waited for; matrix products, arithmetic and copies ran while one was open for 13% of the time, Pallas kernels for 0%

profile of v1, /device:TPU:8, one launch (start us, length us, event | category | flops | bytes accessed | tf_op | source)
XLA Modules:
  0.0 407.9 jit_solution(17727695553102807954)
XLA Ops:
  8.0 3.4 collective-permute-start.2
  13.6 3.6 collective-permute-done.3
  17.9 2.0 copy.42
  20.0 2.5 reshape.135
  22.5 7.3 %all-to-all-start.1 = ((bf16[16,2,3456]{2,1,0:T(2,128)(2,1)}), bf16[16,2,3456]{2,1,0:T(2,128)(2,1)S(1)}, u32[]{:S(2)}, u32[]{:S(2)}) async-start(bf16[16,2,3456]{2,1,0:T(2,128)(2,1)} %reshape.135), calls=%async_computation.1 | async-start | bytes 442368 | tf_op jit(solution)/shard_map/all_to_all | solution.py:50
  30.6 4.2 %collective-permute-start = (bf16[1,16,1024]{2,1,0:T(8,128)(2,1)S(1)}, bf16[1,16,1024]{2,1,0:T(8,128)(2,1)S(1)}, u32[]{:S(2)}, u32[]{:S(2)}) collective-permute-start(bf16[1,16,1024]{2,1,0:T(8,128)(2,1)S(1)} %slice.120), channel_id=1, source_target_pairs={{0,16},{16,32},{32,48},{48,64},{64,80},{80,96},{96,112},{112,128},... | collective-permute-start | bytes 98312 | tf_op jit(solution)/shard_map/ppermute | solution.py:18
  37.0 3.6 collective-permute-done.1
  40.7 1.6 stack.2
  42.2 7.8 %all-to-all-start = ((bf16[16,4,16,1024]{3,2,1,0:T(8,128)(2,1)}), bf16[16,4,16,1024]{3,2,1,0:T(8,128)(2,1)S(1)}, u32[]{:S(2)}, u32[]{:S(2)}) async-start(bf16[16,4,16,1024]{3,2,1,0:T(8,128)(2,1)} %stack.2), calls=%async_computation | async-start | bytes 4194304 | tf_op jit(solution)/shard_map/all_to_all | solution.py:10
  52.9 3.5 reshape.136
  56.4 4.8 %copy.51 = bf16[27,16,16,16]{3,2,1,0:T(8,128)(2,1)} copy(bf16[27,16,16,16]{0,1,3,2:T(8,128)(2,1)S(1)} %bitcast.88) | data formatting | bytes 442368 | tf_op jit(solution)/shard_map/all_to_all | solution.py:50
  61.2 2.6 fusion.79
  63.9 2.6 copy.48
  66.5 1.6 slice.157
  68.2 1.6 copy.46
  69.8 1.6 slice.154
  72.8 8.9 %all-to-all-done = bf16[16,4,16,1024]{3,2,1,0:T(8,128)(2,1)S(1)} async-done(((bf16[16,4,16,1024]{3,2,1,0:T(8,128)(2,1)}), bf16[16,4,16,1024]{3,2,1,0:T(8,128)(2,1)S(1)}, u32[]{:S(2)}, u32[]{:S(2)}) %all-to-all-start) | async-done | bytes 2097184 | tf_op jit(solution)/shard_map/all_to_all | solution.py:10
  83.0 1.8 copy.38
  84.8 5.0 %all-gather.2.cloned.1.call-done = bf16[4,256,1024]{2,1,0:T(8,128)(2,1)} async-done(((bf16[4,16,1024]{2,1,0:T(8,128)(2,1)}), bf16[4,256,1024]{2,1,0:T(8,128)(2,1)}) %all-gather.2.cloned.1.call-update) | async-done | bytes 2097168 | tf_op jit(solution)/shard_map/all_gather | solution.py:72
  89.8 2.5 fusion.29
  95.9 6.5 %copy-done.3 = bf16[4,2304,1024]{2,1,0:T(8,128)(2,1)} copy-done((bf16[4,2304,1024]{2,1,0:T(8,128)(2,1)}, bf16[4,2304,1024]{2,1,0:T(8,128)(2,1)S(1)}, u32[]{:S(2)}) %copy-start.3) | copy-done | bytes 18874392
  102.3 3.1 fusion.37
  105.5 2.9 fusion.39
  108.3 2.3 fusion.41
  111.9 3.9 fusion.43
  120.4 2.5 convolution_bitcast_fusion.2
  122.9 2.8 convolution_bitcast_fusion.1
  126.8 2.5 convolution_bitcast_fusion
  130.4 5.0 %fusion = f32[2,1024,16]{1,2,0:T(8,128)S(1)} fusion(bf16[16,2304,1]{1,0,2:T(8,128)(2,1)S(1)} %reshape.125, bf16[4,2304,1024]{2,1,0:T(8,128)(2,1)} %get-tuple-element.22), kind=kOutput, calls=%fused_computation | convolution fusion | flops 150994944 | bytes 9641984 | tf_op jit(solution)/shard_map/kj,zjp->zkp/dot_general | solution.py:79
  135.4 5.2 %fusion.2 = f32[2,1024,16]{1,2,0:T(8,128)S(1)} fusion(bf16[16,2304,1]{1,0,2:T(8,128)(2,1)S(1)} %reshape.124, bf16[4,2304,1024]{2,1,0:T(8,128)(2,1)} %get-tuple-element.22), kind=kOutput, calls=%fused_computation.2 | convolution fusion | flops 150994944 | bytes 9641984 | tf_op jit(solution)/shard_map/kj,zjp->zkp/dot_general | solution.py:79
  140.6 5.8 %fusion.56 = bf16[2,1024,16]{1,2,0:T(8,128)(2,1)S(1)} fusion(f32[2,1024,16]{1,2,0:T(8,128)S(1)} %fusion, f32[2,1024,16]{1,2,0:T(8,128)S(1)} %fusion.2, bf16[16,2304,1]{1,0,2:T(8,128)(2,1)S(1)} %reshape.123, bf16[4,2304,1024]{2,1,0:T(8,128)(2,1)} %get-tuple-element.22), kind=kOutput, calls=%fused_computation.69 | convolution fusion | flops 151093248 | bytes 9838592 | tf_op jit(solution)/shard_map/kj,zjp->zkp/dot_general | solution.py:79
  151.9 246.8 %all-reduce.4.cloned.1.call-done = f32[27,16,256]{2,0,1:T(8,128)} async-done(((f32[27,16,256]{2,0,1:T(8,128)}), f32[27,16,256]{2,0,1:T(8,128)}) %all-reduce.4.cloned.1.call-update) | async-done | bytes 442384 | tf_op jit(solution)/shard_map/psum | solution.py:82
  (79 shorter events, 31.4 us)
Async XLA Ops:
  7.2 82.6 %all-gather.2.cloned.1.call-start = ((), (), s32[]{:S(2)}) async-start(), calls=%async_computation.2 | async-start | bytes 2228224 | tf_op jit(solution)/shard_map/all_gather | solution.py:72
  8.0 5.6 %collective-permute-start.2 = (bf16[1,16,1024]{2,1,0:T(8,128)(2,1)S(1)}, bf16[1,16,1024]{2,1,0:T(8,128)(2,1)S(1)}, u32[]{:S(2)}, u32[]{:S(2)}) collective-permute-start(bf16[1,16,1024]{2,1,0:T(8,128)(2,1)S(1)} %slice.138), channel_id=1, source_target_pairs={{0,16},{16,32},{32,48},{48,64},{64,80},{80,96},{96,112},{112,128},... | collective-permute-start | bytes 98312 | tf_op jit(solution)/shard_map/ppermute | solution.py:18
  11.4 5.8 %collective-permute-start.3 = (bf16[1,16,1024]{2,1,0:T(8,128)(2,1)S(1)}, bf16[1,16,1024]{2,1,0:T(8,128)(2,1)S(1)}, u32[]{:S(2)}, u32[]{:S(2)}) collective-permute-start(bf16[1,16,1024]{2,1,0:T(8,128)(2,1)S(1)} %slice.140), channel_id=1, source_target_pairs={{16,0},{32,16},{48,32},{64,48},{80,64},{96,80},{112,96},{128,112},... | collective-permute-start | bytes 98312 | tf_op jit(solution)/shard_map/ppermute | solution.py:21
  19.9 30.2 %copy-start.5 = (bf16[27,16,256]{2,1,0:T(8,128)(2,1)S(1)}, bf16[27,16,256]{2,1,0:T(8,128)(2,1)}, u32[]{:S(2)}) copy-start(bf16[27,16,256]{2,1,0:T(8,128)(2,1)} %param.4) | copy-start | bytes 663556
  22.5 18.2 %all-to-all-start.1 = ((bf16[16,2,3456]{2,1,0:T(2,128)(2,1)}), bf16[16,2,3456]{2,1,0:T(2,128)(2,1)S(1)}, u32[]{:S(2)}, u32[]{:S(2)}) async-start(bf16[16,2,3456]{2,1,0:T(2,128)(2,1)} %reshape.135), calls=%async_computation.1 | async-start | bytes 442368 | tf_op jit(solution)/shard_map/all_to_all | solution.py:50
  30.6 6.4 %collective-permute-start = (bf16[1,16,1024]{2,1,0:T(8,128)(2,1)S(1)}, bf16[1,16,1024]{2,1,0:T(8,128)(2,1)S(1)}, u32[]{:S(2)}, u32[]{:S(2)}) collective-permute-start(bf16[1,16,1024]{2,1,0:T(8,128)(2,1)S(1)} %slice.120), channel_id=1, source_target_pairs={{0,16},{16,32},{32,48},{48,64},{64,80},{80,96},{96,112},{112,128},... | collective-permute-start | bytes 98312 | tf_op jit(solution)/shard_map/ppermute | solution.py:18
  34.8 5.8 %collective-permute-start.1 = (bf16[1,16,1024]{2,1,0:T(8,128)(2,1)S(1)}, bf16[1,16,1024]{2,1,0:T(8,128)(2,1)S(1)}, u32[]{:S(2)}, u32[]{:S(2)}) collective-permute-start(bf16[1,16,1024]{2,1,0:T(8,128)(2,1)S(1)} %slice.122), channel_id=1, source_target_pairs={{16,0},{32,16},{48,32},{64,48},{80,64},{96,80},{112,96},{128,112},... | collective-permute-start | bytes 98312 | tf_op jit(solution)/shard_map/ppermute | solution.py:21
  40.7 11.6 %copy-start.6 = (bf16[16,2,3456]{2,1,0:T(2,128)(2,1)}, bf16[16,2,3456]{2,1,0:T(2,128)(2,1)S(1)}, u32[]{:S(2)}) copy-start(bf16[16,2,3456]{2,1,0:T(2,128)(2,1)S(1)} %all-to-all-done.1) | copy-start | bytes 663556
  42.2 39.5 %all-to-all-start = ((bf16[16,4,16,1024]{3,2,1,0:T(8,128)(2,1)}), bf16[16,4,16,1024]{3,2,1,0:T(8,128)(2,1)S(1)}, u32[]{:S(2)}, u32[]{:S(2)}) async-start(bf16[16,4,16,1024]{3,2,1,0:T(8,128)(2,1)} %stack.2), calls=%async_computation | async-start | bytes 4194304 | tf_op jit(solution)/shard_map/all_to_all | solution.py:10
  50.1 348.7 %all-reduce.4.cloned.1.call-start = ((), (), s32[]{:S(2)}) async-start(), calls=%async_computation.3 | async-start | bytes 1048576 | tf_op jit(solution)/shard_map/psum | solution.py:82
  81.7 1.3 copy-start.4
  84.8 8.0 %copy-start.10 = (bf16[1024]{0:T(1024)(128)(2,1)S(1)}, bf16[1024]{0:T(1024)(128)(2,1)}, u32[]{:S(2)}) copy-start(bf16[1024]{0:T(1024)(128)(2,1)} %fusion.75) | copy-start | bytes 6148
  89.8 2.5 copy-start.2
  95.9 6.5 %copy-start.3 = (bf16[4,2304,1024]{2,1,0:T(8,128)(2,1)}, bf16[4,2304,1024]{2,1,0:T(8,128)(2,1)S(1)}, u32[]{:S(2)}) copy-start(bf16[4,2304,1024]{2,1,0:T(8,128)(2,1)S(1)} %multiply_dynamic-update-slice_fusion) | copy-start | bytes 56623108
  120.4 6.4 %copy-start = (bf16[4,2304,1024]{2,1,0:T(8,128)(2,1)}, bf16[4,2304,1024]{2,1,0:T(8,128)(2,1)S(1)}, u32[]{:S(2)}) copy-start(bf16[4,2304,1024]{2,1,0:T(8,128)(2,1)S(1)} %fusion.27) | copy-start | bytes 56623108
  135.4 11.7 %copy-start.1 = (bf16[4,2304,1024]{2,1,0:T(8,128)(2,1)S(1)}, bf16[4,2304,1024]{2,1,0:T(8,128)(2,1)}, u32[]{:S(2)}) copy-start(bf16[4,2304,1024]{2,1,0:T(8,128)(2,1)} %copy-done) | copy-start | bytes 56623108
  140.6 6.7 %copy-start.7 = (bf16[16,2304,1]{1,0,2:T(8,128)(2,1)S(1)}, bf16[16,2304,1]{1,0,2:T(8,128)(2,1)}, u32[]{:S(2)}) copy-start(bf16[16,2304,1]{1,0,2:T(8,128)(2,1)} %reshape.121) | copy-start | bytes 221188
  147.2 1.3 copy-start.8
  148.6 1.4 copy-start.9
Sparse Core Ops, SparseCore 0:
  18.1 71.6 all-gather.1
  130.5 268.1 all-reduce.3
